TPU v7x, 32 devices: a whole 2x2x4 slice. The times are simulated.
32 devices in a mesh: tp: 4 (over y, core), fsdp: 8 (over z, x).
Axes of the slice: x: 2, y: 2, z: 4, core: 2. Of those that a mesh axis runs over, the one named last changes fastest.
Arguments:
- momentum: float32 [8192, 28672], P('tp', 'fsdp'), may hold values from -6 to 6
- gradient: bfloat16 [8192, 28672], P('tp', 'fsdp'), may hold values from -6 to 6
- basis: float32 [28672, 512], P('fsdp', 'tp'), may hold values from -1 to 1
Outputs:
- new_momentum: float32 [8192, 28672], P('tp', 'fsdp')
- new_basis: float32 [28672, 512], P('fsdp', 'tp')
- left_factor: float32 [8192, 512], P(('tp', 'fsdp'))
All inputs are finite; a program needn't handle non-finite values.
Results may differ from a plain program's by a relative error of at most 0.0003.
Values sent between devices are 32-bit elements; how exact they have to be, the bound alone decides.
A program may use at most 192 MiB of HBM per device.

v0:
```python
import jax
import jax.numpy as jnp
from jax import lax
from jax.sharding import PartitionSpec as P

keep_rate = 0.95
tiny = 1e-06
high = lax.Precision.HIGHEST


def solve_right(left, gram):
    lower = jnp.linalg.cholesky(gram)
    return jax.scipy.linalg.solve_triangular(lower, left.T, lower=True).T


def local_gram(left):
    return jnp.dot(left.T, left, precision=high, preferred_element_type=jnp.float32)


def gram_over_rows(left):
    return lax.psum(local_gram(left), "tp")


def on_device(momentum, gradient, basis):
    tile = momentum + gradient.astype(jnp.float32)
    partial_value = jnp.dot(
        tile,
        lax.all_gather(basis, "tp", axis=1, tiled=True),
        precision=high,
        preferred_element_type=jnp.float32,
    )
    share_rows = tile.shape[0] // lax.axis_size("fsdp")
    whole = lax.psum(partial_value, "fsdp")
    for turn in range(2):
        whole = solve_right(whole, gram_over_rows(whole))
    own_left = lax.dynamic_slice_in_dim(whole, lax.axis_index("fsdp") * share_rows, share_rows, 0)
    partial_right = jnp.dot(tile.T, whole, precision=high, preferred_element_type=jnp.float32)
    mine = lax.psum_scatter(partial_right, "tp", scatter_dimension=1, tiled=True)
    squares = lax.psum(jnp.sum(mine * mine, axis=0), "fsdp")
    new_basis = mine / jnp.sqrt(squares + tiny)[None, :]
    full_right = lax.all_gather(mine, "tp", axis=1, tiled=True)
    new_momentum = tile - (1.0 - keep_rate) * jnp.dot(
        whole, full_right.T, precision=high, preferred_element_type=jnp.float32
    )
    return (new_momentum, new_basis, own_left)


def solution(mesh):
    placed = (P("tp", "fsdp"), P("tp", "fsdp"), P("fsdp", "tp"))
    return jax.shard_map(
        on_device,
        mesh=mesh,
        in_specs=placed,
        out_specs=(P("tp", "fsdp"), P("fsdp", "tp"), P(("tp", "fsdp"), None)),
        check_vma=False,
    )
```

profile of v0, /device:TPU:0, one launch (start us, length us, event | category | flops | bytes accessed | tf_op | source)
XLA Modules:
  0.0 1009.8 jit_solution(1744838277263823175)
XLA Ops:
  7.9 57.6 %all-gather.3.cloned.1.call-done = f32[3584,512]{1,0:T(8,128)} async-done(((f32[3584,128]{1,0:T(8,128)}), f32[3584,512]{1,0:T(8,128)}) %all-gather.3.cloned.1.call-update) | async-done | bytes 7340048 | tf_op jit(solution)/shard_map/all_gather | solution.py:28
  65.6 53.8 %fusion.1 = f32[2048,512]{1,0:T(8,128)} fusion(f32[3584,512]{1,0:T(8,128)} %all-gather.3.cloned.1.call-done, f32[2048,3584]{1,0:T(8,128)} %param.6, bf16[2048,3584]{1,0:T(8,128)(2,1)} %param.7), kind=kOutput, calls=%fused_computation.7 | convolution fusion | flops 45111836672 | bytes 55574528 | tf_op jit(solution)/shard_map/dot_general | solution.py:26
  119.4 156.5 %all-reduce.5.cloned.1.call-done = f32[2048,512]{1,0:T(8,128)} async-done(((f32[2048,512]{1,0:T(8,128)}), f32[2048,512]{1,0:T(8,128)}) %all-reduce.5.cloned.1.call-update) | async-done | bytes 4194320 | tf_op jit(solution)/shard_map/psum | solution.py:33
  275.9 11.4 %fusion.88 = f32[512,512]{0,1:T(8,128)} fusion(f32[2048,512]{1,0:T(8,128)} %all-reduce.5.cloned.1.call-done), kind=kOutput, calls=%fused_computation.151 | convolution fusion | flops 6442450944 | bytes 5242880 | tf_op jit(solution)/shard_map/dot_general | solution.py:17
  287.8 34.9 %all-reduce.7.cloned.1.call-done = f32[512,512]{0,1:T(8,128)} async-done(((f32[512,512]{0,1:T(8,128)}), f32[512,512]{0,1:T(8,128)}) %all-reduce.7.cloned.1.call-update) | async-done | bytes 1048592 | tf_op jit(solution)/shard_map/psum | solution.py:21
  325.8 11.7 %cholesky.286 = f32[128,128]{1,0:T(8,128)S(1)} custom-call(f32[128,128]{1,0:T(8,128)S(1)} %cholesky.426), custom_call_target="Cholesky" | custom-call | tf_op jit(solution)/shard_map/jit(cholesky)/cholesky | solution.py:12
  348.2 11.7 %cholesky.305 = f32[128,128]{1,0:T(8,128)S(1)} custom-call(f32[128,128]{1,0:T(8,128)S(1)} %cholesky.430), custom_call_target="Cholesky" | custom-call | tf_op jit(solution)/shard_map/jit(cholesky)/cholesky | solution.py:12
  359.9 10.0 custom-call.28
  370.5 11.7 %cholesky.326 = f32[128,128]{1,0:T(8,128)S(1)} custom-call(f32[128,128]{1,0:T(8,128)S(1)} %cholesky.435), custom_call_target="Cholesky" | custom-call | tf_op jit(solution)/shard_map/jit(cholesky)/cholesky | solution.py:12
  392.7 11.7 %cholesky.343 = f32[128,128]{1,0:T(8,128)S(1)} custom-call(f32[128,128]{1,0:T(8,128)S(1)} %convolution_subtract_fusion.9), custom_call_target="Cholesky" | custom-call | tf_op jit(solution)/shard_map/jit(cholesky)/cholesky | solution.py:12
  417.3 39.3 %custom-call.30 = f32[4,128,128]{1,2,0:T(8,128)S(1)} custom-call(f32[4,128,128]{2,1,0:T(8,128)S(1)} %get-tuple-element.19), custom_call_target="InvertDiagBlocksLowerTriangular" | custom-call | tf_op jit(solution)/shard_map/jit(_solve_triangular)/triangular_solve | solution.py:13
  483.7 36.7 %all-reduce.9.cloned.1.call-done = f32[512,512]{0,1:T(8,128)} async-done(((f32[512,512]{0,1:T(8,128)}), f32[512,512]{0,1:T(8,128)}) %all-reduce.9.cloned.1.call-update) | async-done | bytes 1048592 | tf_op jit(solution)/shard_map/psum | solution.py:21
  524.4 11.7 %cholesky.358 = f32[128,128]{1,0:T(8,128)S(1)} custom-call(f32[128,128]{1,0:T(8,128)S(1)} %cholesky.439), custom_call_target="Cholesky" | custom-call | tf_op jit(solution)/shard_map/jit(cholesky)/cholesky | solution.py:12
  548.6 11.7 %cholesky.377 = f32[128,128]{1,0:T(8,128)S(1)} custom-call(f32[128,128]{1,0:T(8,128)S(1)} %cholesky.443), custom_call_target="Cholesky" | custom-call | tf_op jit(solution)/shard_map/jit(cholesky)/cholesky | solution.py:12
  560.4 10.0 custom-call.32
  572.0 11.7 %cholesky.398 = f32[128,128]{1,0:T(8,128)S(1)} custom-call(f32[128,128]{1,0:T(8,128)S(1)} %cholesky.448), custom_call_target="Cholesky" | custom-call | tf_op jit(solution)/shard_map/jit(cholesky)/cholesky | solution.py:12
  595.0 11.7 %cholesky.415 = f32[128,128]{1,0:T(8,128)S(1)} custom-call(f32[128,128]{1,0:T(8,128)S(1)} %convolution_subtract_fusion.8), custom_call_target="Cholesky" | custom-call | tf_op jit(solution)/shard_map/jit(cholesky)/cholesky | solution.py:12
  613.5 11.7 %while.5 = (s32[]{:T(128)}, f32[512,512]{1,0:T(8,128)}, s32[4,2]{0,1:T(2,128)S(1)}, f32[4,128,128]{2,1,0:T(8,128)S(1)}, s32[]{:T(128)}) while((s32[]{:T(128)}, f32[512,512]{1,0:T(8,128)}, s32[4,2]{0,1:T(2,128)S(1)}, f32[4,128,128]{2,1,0:T(8,128)S(1)}, s32[]{:T(128)}) %tuple.74), condition=%wide.while_cond.clone, body=%wide.while_body.clone.sunk | while | flops 2 | bytes 131189 | solution.py:13
  625.2 39.3 %custom-call.34 = f32[4,128,128]{1,2,0:T(8,128)S(1)} custom-call(f32[4,128,128]{2,1,0:T(8,128)S(1)} %get-tuple-element.20), custom_call_target="InvertDiagBlocksLowerTriangular" | custom-call | tf_op jit(solution)/shard_map/jit(_solve_triangular)/triangular_solve | solution.py:13
  677.2 107.3 %fusion = f32[3584,512]{1,0:T(8,128)} fusion(f32[2048,3584]{1,0:T(8,128)} %param.6, bf16[2048,3584]{1,0:T(8,128)(2,1)} %param.7, f32[128,2048]{1,0:T(8,128)S(1)} %fusion.54, f32[128,2048]{1,0:T(8,128)S(1)} %fusion.55, f32[128,2048]{1,0:T(8,128)S(1)} %fusion.57, f32[128,2048]{1,0:T(8,128)S(1)} %fusion.58), kind=kOutput, calls=%fused_computation.6 | convolution fusion | flops 45114982400 | bytes 55574528 | tf_op jit(solution)/shard_map/dot_general | solution.py:37
  784.6 65.2 %reduce-scatter.2.cloned.1.call-done = f32[3584,128]{1,0:T(8,128)} async-done(((f32[3584,512]{1,0:T(8,128)}), f32[3584,128]{1,0:T(8,128)}) %reduce-scatter.2.cloned.1.call-update) | async-done | bytes 1835024 | tf_op jit(solution)/shard_map/reduce_scatter | solution.py:38
  856.2 21.4 %psum.31 = f32[128]{0:T(128)S(1)} all-reduce(f32[128]{0:T(128)S(1)} %multiply_reduce_fusion), channel_id=1, replica_groups=mesh['tp'=4,'fsdp'=8] {'fsdp'}, use_global_device_ids=true, to_apply=%region_13.16 | all-reduce | flops 128 | bytes 1024 | tf_op jit(solution)/shard_map/psum | solution.py:39
  880.4 24.1 %all-gather.5.cloned.1.call-done = f32[3584,512]{1,0:T(8,128)} async-done(((f32[3584,128]{1,0:T(8,128)}), f32[3584,512]{1,0:T(8,128)}) %all-gather.5.cloned.1.call-update) | async-done | bytes 7340048 | tf_op jit(solution)/shard_map/all_gather | solution.py:41
  904.5 98.3 %multiply_subtract_fusion = f32[2048,3584]{1,0:T(8,128)} fusion(f32[3584,512]{1,0:T(8,128)} %all-gather.5.cloned.1.call-done, f32[2048,3584]{1,0:T(8,128)} %param.6, bf16[2048,3584]{1,0:T(8,128)(2,1)} %param.7, f32[128,2048]{1,0:T(8,128)} %copy-done.2, f32[128,2048]{1,0:T(8,128)S(1)} %fusion.55, f32[128,2048]{1,0:T(8,128)S(1)} %fusion.57, ...), kind=kOutput, calls=%fused_computation.4 | convolution fusion | flops 45129662464 | bytes 84934656 | tf_op jit(solution)/shard_map/dot_general | solution.py:42
  (119 shorter events, 138.2 us)
Async XLA Ops:
  7.2 58.4 %all-gather.3.cloned.1.call-start = ((), (), s32[]{:S(2)}) async-start(), calls=%async_computation.1 | async-start | bytes 9175040 | tf_op jit(solution)/shard_map/all_gather | solution.py:28
  7.9 268.0 %all-reduce.5.cloned.1.call-start = ((), (), s32[]{:S(2)}) async-start(), calls=%async_computation.2 | async-start | bytes 8388608 | tf_op jit(solution)/shard_map/psum | solution.py:33
  119.4 203.4 %all-reduce.7.cloned.1.call-start = ((), (), s32[]{:S(2)}) async-start(), calls=%async_computation.3 | async-start | bytes 2097152 | tf_op jit(solution)/shard_map/psum | solution.py:21
  287.3 233.1 %all-reduce.9.cloned.1.call-start = ((), (), s32[]{:S(2)}) async-start(), calls=%async_computation.4 | async-start | bytes 2097152 | tf_op jit(solution)/shard_map/psum | solution.py:21
  456.7 6.6 copy-start
  467.9 6.9 copy-start.1
  474.7 1.0 copy-start.3
  483.5 366.2 %reduce-scatter.2.cloned.1.call-start = ((), (), s32[]{:S(2)}) async-start(), calls=%async_computation.5 | async-start | bytes 9175040 | tf_op jit(solution)/shard_map/reduce_scatter | solution.py:38
  523.4 1.0 copy-start.5
  667.5 4.7 copy-start.4
  676.2 1.0 copy-start.2
  784.5 119.9 %all-gather.5.cloned.1.call-start = ((), (), s32[]{:S(2)}) async-start(), calls=%async_computation.6 | async-start | bytes 9175040 | tf_op jit(solution)/shard_map/all_gather | solution.py:41
Sparse Core Ops, SparseCore 0:
  9.5 56.0 all-gather.2
  119.5 156.3 all-reduce.4
  287.4 35.2 all-reduce.6
  483.6 36.7 all-reduce.8
  784.6 65.0 reduce-scatter.1
  851.1 53.2 all-gather.4
where the time goes:
time: 1020 us; the launch traced here: 1010 us
  waiting for transfers between devices  376 us (37%)
  matrix products  315 us (31%)
  other arithmetic  247 us (24%)
  local copies, waits for them, and re-layouts  28.8 us (3%)
  blocking collectives  21.4 us (2%)
  between operations  20 us (2%)
    another operation x29, other arithmetic, solve_right(): lower = jnp.linalg.cholesky(gram)  158 us
    psum x1, waiting for transfers between devices, on_device(): whole = lax.psum(partial_value, 'fsdp')  156 us
    dot_general x1, matrix products, on_device(): jnp.dot(tile.T, whole, precision=high, preferred_element_type=jnp.float32)  107 us
    dot_general x1, matrix products, on_device(): jnp.dot(whole, full_right.T, precision=high, preferred_element_type=jnp.f...  98.3 us
    another operation x6, other arithmetic, solve_right(): return jax.scipy.linalg.solve_triangular(lower, left.T, lower=True).T  81.9 us
    psum x2, waiting for transfers between devices, gram_over_rows(): return lax.psum(local_gram(left), 'tp')  71.6 us
    reduce_scatter x1, waiting for transfers between devices, on_device(): lax.psum_scatter(partial_right, 'tp', scatter_dimension=1, tiled=True)  65.2 us
    all_gather x1, waiting for transfers between devices, on_device(): lax.all_gather(basis, 'tp', axis=1, tiled=True)  57.6 us
  transfers between devices with their start and end apart: 6, of which 6 were waited for; matrix products, arithmetic and copies ran while one was open for 1% of the time, Pallas kernels for 0%

commit v1 on v0

--- a/solution.py
+++ b/solution.py
@@ -30,7 +30,9 @@
         preferred_element_type=jnp.float32,
     )
     share_rows = tile.shape[0] // lax.axis_size("fsdp")
-    whole = lax.psum(partial_value, "fsdp")
+    whole = partial_value
+    for hop in (1, 2, 4):
+        whole = whole + lax.ppermute(whole, "fsdp", [(dev, dev ^ hop) for dev in range(8)])
     for turn in range(2):
         whole = solve_right(whole, gram_over_rows(whole))
     own_left = lax.dynamic_slice_in_dim(whole, lax.axis_index("fsdp") * share_rows, share_rows, 0)

time: 1020 us -> 1250 us (1.23)
  waiting for transfers between devices: 376 us -> 576 us
  matrix products: 315 us -> 330 us
    ppermute x0 -> x3, waiting for transfers between devices: none -> 361 us  [on_device(): lax.ppermute(whole, 'fsdp', [(dev, dev ^ hop) for dev in range(8)])]
    psum x1 -> x0, waiting for transfers between devices: 156 us -> none  [on_device(): whole = lax.psum(partial_value, 'fsdp')]
    dot_general x2, matrix products: 19.2 us -> 32.6 us  [local_gram(): jnp.dot(left.T, left, precision=high, preferred_element_type=jnp.float32)]
  transfers between devices with their start and end apart: 6 -> 8, of which waited for: 6 -> 8; matrix products, arithmetic and copies ran while one was open for 1% -> 1% of each run, Pallas kernels for 0% -> 0%
where the time goes in v1:
time: 1250 us; the launch traced here: 1240 us
  waiting for transfers between devices  576 us (46%)
  matrix products  330 us (26%)
  other arithmetic  258 us (21%)
  local copies, waits for them, and re-layouts  29.3 us (2%)
  blocking collectives  21.4 us (2%)
  between operations  19.5 us (2%)
    ppermute x3, waiting for transfers between devices, on_device(): lax.ppermute(whole, 'fsdp', [(dev, dev ^ hop) for dev in range(8)])  361 us
    another operation x29, other arithmetic, solve_right(): lower = jnp.linalg.cholesky(gram)  158 us
    dot_general x1, matrix products, on_device(): jnp.dot(tile.T, whole, precision=high, preferred_element_type=jnp.float32)  107 us
    dot_general x1, matrix products, on_device(): jnp.dot(whole, full_right.T, precision=high, preferred_element_type=jnp.f...  98.3 us
    another operation x6, other arithmetic, solve_right(): return jax.scipy.linalg.solve_triangular(lower, left.T, lower=True).T  81.9 us
    psum x2, waiting for transfers between devices, gram_over_rows(): return lax.psum(local_gram(left), 'tp')  66.6 us
    reduce_scatter x1, waiting for transfers between devices, on_device(): lax.psum_scatter(partial_right, 'tp', scatter_dimension=1, tiled=True)  65.2 us
    all_gather x1, waiting for transfers between devices, on_device(): lax.all_gather(basis, 'tp', axis=1, tiled=True)  57.6 us
  transfers between devices with their start and end apart: 8, of which 8 were waited for; matrix products, arithmetic and copies ran while one was open for 1% of the time, Pallas kernels for 0%

profile of v1, /device:TPU:0, one launch (start us, length us, event | category | flops | bytes accessed | tf_op | source)
XLA Modules:
  0.0 1240.1 jit_solution(7234896255357869918)
XLA Ops:
  7.9 57.6 %all-gather.3.cloned.1.call-done = f32[3584,512]{1,0:T(8,128)} async-done(((f32[3584,128]{1,0:T(8,128)}), f32[3584,512]{1,0:T(8,128)}) %all-gather.3.cloned.1.call-update) | async-done | bytes 7340048 | tf_op jit(solution)/shard_map/all_gather | solution.py:28
  65.6 56.1 %fusion.1 = f32[2048,512]{1,0:T(8,128)S(1)} fusion(f32[3584,512]{1,0:T(8,128)} %all-gather.3.cloned.1.call-done, f32[2048,3584]{1,0:T(8,128)} %param.6, bf16[2048,3584]{1,0:T(8,128)(2,1)} %param.7), kind=kOutput, calls=%fused_computation.7 | convolution fusion | flops 45111836672 | bytes 55574528 | tf_op jit(solution)/shard_map/dot_general | solution.py:26
  123.2 91.3 %collective-permute-done = f32[2048,512]{1,0:T(8,128)S(1)} collective-permute-done((f32[2048,512]{1,0:T(8,128)S(1)}, f32[2048,512]{1,0:T(8,128)S(1)}, u32[]{:S(2)}, u32[]{:S(2)}) %collective-permute-start) | collective-permute-done | bytes 4194336 | tf_op jit(solution)/shard_map/ppermute | solution.py:35
  217.1 90.4 %collective-permute-done.1 = f32[2048,512]{1,0:T(8,128)S(1)} collective-permute-done((f32[2048,512]{1,0:T(8,128)S(1)}, f32[2048,512]{1,0:T(8,128)S(1)}, u32[]{:S(2)}, u32[]{:S(2)}) %collective-permute-start.1) | collective-permute-done | bytes 4194336 | tf_op jit(solution)/shard_map/ppermute | solution.py:35
  312.9 179.7 %collective-permute-done.2 = f32[2048,512]{1,0:T(8,128)} collective-permute-done((f32[2048,512]{1,0:T(8,128)}, f32[2048,512]{1,0:T(8,128)}, u32[]{:S(2)}, u32[]{:S(2)}) %collective-permute-start.2) | collective-permute-done | bytes 4194336 | tf_op jit(solution)/shard_map/ppermute | solution.py:35
  492.6 24.8 %fusion.32 = f32[512,512]{0,1:T(8,128)} fusion(f32[2048,512]{1,0:T(8,128)} %add.63, f32[2048,512]{1,0:T(8,128)} %collective-permute-done.2), kind=kOutput, calls=%fused_computation.40 | convolution fusion | flops 6443499520 | bytes 9437184 | tf_op jit(solution)/shard_map/dot_general | solution.py:17
  523.9 29.9 %all-reduce.4.cloned.1.call-done = f32[512,512]{0,1:T(8,128)} async-done(((f32[512,512]{0,1:T(8,128)}), f32[512,512]{0,1:T(8,128)}) %all-reduce.4.cloned.1.call-update) | async-done | bytes 1048592 | tf_op jit(solution)/shard_map/psum | solution.py:21
  556.8 11.7 cholesky.286
  579.2 11.7 cholesky.305
  601.8 11.7 cholesky.326
  624.0 11.9 cholesky.343
  649.1 39.3 %custom-call.30 = f32[4,128,128]{1,2,0:T(8,128)S(1)} custom-call(f32[4,128,128]{2,1,0:T(8,128)S(1)} %get-tuple-element.19), custom_call_target="InvertDiagBlocksLowerTriangular" | custom-call | tf_op jit(solution)/shard_map/jit(_solve_triangular)/triangular_solve | solution.py:13
  714.4 36.7 %all-reduce.6.cloned.1.call-done = f32[512,512]{0,1:T(8,128)} async-done(((f32[512,512]{0,1:T(8,128)}), f32[512,512]{0,1:T(8,128)}) %all-reduce.6.cloned.1.call-update) | async-done | bytes 1048592 | tf_op jit(solution)/shard_map/psum | solution.py:21
  755.1 11.7 cholesky.358
  779.3 11.7 cholesky.377
  802.6 11.7 cholesky.398
  825.6 11.7 cholesky.415
  844.2 11.7 while.5
  855.9 39.3 %custom-call.34 = f32[4,128,128]{1,2,0:T(8,128)S(1)} custom-call(f32[4,128,128]{2,1,0:T(8,128)S(1)} %get-tuple-element.20), custom_call_target="InvertDiagBlocksLowerTriangular" | custom-call | tf_op jit(solution)/shard_map/jit(_solve_triangular)/triangular_solve | solution.py:13
  907.8 107.3 %fusion = f32[3584,512]{1,0:T(8,128)} fusion(f32[2048,3584]{1,0:T(8,128)} %param.6, bf16[2048,3584]{1,0:T(8,128)(2,1)} %param.7, f32[128,2048]{1,0:T(8,128)S(1)} %fusion.57, f32[128,2048]{1,0:T(8,128)S(1)} %fusion.58, f32[128,2048]{1,0:T(8,128)S(1)} %fusion.60, f32[128,2048]{1,0:T(8,128)S(1)} %fusion.61), kind=kOutput, calls=%fused_computation.6 | convolution fusion | flops 45114982400 | bytes 55574528 | tf_op jit(solution)/shard_map/dot_general | solution.py:39
  1015.2 65.2 %reduce-scatter.2.cloned.1.call-done = f32[3584,128]{1,0:T(8,128)} async-done(((f32[3584,512]{1,0:T(8,128)}), f32[3584,128]{1,0:T(8,128)}) %reduce-scatter.2.cloned.1.call-update) | async-done | bytes 1835024 | tf_op jit(solution)/shard_map/reduce_scatter | solution.py:40
  1086.8 21.4 %psum.23 = f32[128]{0:T(128)S(1)} all-reduce(f32[128]{0:T(128)S(1)} %multiply_reduce_fusion), channel_id=1, replica_groups=mesh['tp'=4,'fsdp'=8] {'fsdp'}, use_global_device_ids=true, to_apply=%region_12.15 | all-reduce | flops 128 | bytes 1024 | tf_op jit(solution)/shard_map/psum | solution.py:41
  1111.0 24.1 %all-gather.5.cloned.1.call-done = f32[3584,512]{1,0:T(8,128)} async-done(((f32[3584,128]{1,0:T(8,128)}), f32[3584,512]{1,0:T(8,128)}) %all-gather.5.cloned.1.call-update) | async-done | bytes 7340048 | tf_op jit(solution)/shard_map/all_gather | solution.py:43
  1135.1 98.3 %multiply_subtract_fusion = f32[2048,3584]{1,0:T(8,128)} fusion(f32[3584,512]{1,0:T(8,128)} %all-gather.5.cloned.1.call-done, f32[2048,3584]{1,0:T(8,128)} %param.6, bf16[2048,3584]{1,0:T(8,128)(2,1)} %param.7, f32[128,2048]{1,0:T(8,128)} %copy-done.2, f32[128,2048]{1,0:T(8,128)S(1)} %fusion.58, f32[128,2048]{1,0:T(8,128)S(1)} %fusion.60, ...), kind=kOutput, calls=%fused_computation.4 | convolution fusion | flops 45129662464 | bytes 84934656 | tf_op jit(solution)/shard_map/dot_general | solution.py:44
  (125 shorter events, 173.8 us)
Async XLA Ops:
  7.2 58.4 %all-gather.3.cloned.1.call-start = ((), (), s32[]{:S(2)}) async-start(), calls=%async_computation.1 | async-start | bytes 9175040 | tf_op jit(solution)/shard_map/all_gather | solution.py:28
  7.9 545.9 %all-reduce.4.cloned.1.call-start = ((), (), s32[]{:S(2)}) async-start(), calls=%async_computation.2 | async-start | bytes 2097152 | tf_op jit(solution)/shard_map/psum | solution.py:21
  121.7 92.8 %collective-permute-start = (f32[2048,512]{1,0:T(8,128)S(1)}, f32[2048,512]{1,0:T(8,128)S(1)}, u32[]{:S(2)}, u32[]{:S(2)}) collective-permute-start(f32[2048,512]{1,0:T(8,128)S(1)} %fusion.1), channel_id=1, source_target_pairs={{0,1},{1,0},{2,3},{3,2},{4,5},{5,4},{6,7},{7,6},{8,9},{9,8},{10,11... | collective-permute-start | bytes 12582920 | tf_op jit(solution)/shard_map/ppermute | solution.py:35
  215.5 91.9 %collective-permute-start.1 = (f32[2048,512]{1,0:T(8,128)S(1)}, f32[2048,512]{1,0:T(8,128)S(1)}, u32[]{:S(2)}, u32[]{:S(2)}) collective-permute-start(f32[2048,512]{1,0:T(8,128)S(1)} %add.62), channel_id=1, source_target_pairs={{0,2},{1,3},{2,0},{3,1},{4,6},{5,7},{6,4},{7,5},{8,10},{9,11},{10,... | collective-permute-start | bytes 12582920 | tf_op jit(solution)/shard_map/ppermute | solution.py:35
  310.5 182.1 %collective-permute-start.2 = (f32[2048,512]{1,0:T(8,128)}, f32[2048,512]{1,0:T(8,128)}, u32[]{:S(2)}, u32[]{:S(2)}) collective-permute-start(f32[2048,512]{1,0:T(8,128)} %add.63), channel_id=1, source_target_pairs={{0,4},{1,5},{2,6},{3,7},{4,0},{5,1},{6,2},{7,3},{8,12},{9,13},{10,... | collective-permute-start | bytes 12582920 | tf_op jit(solution)/shard_map/ppermute | solution.py:35
  517.4 233.7 %all-reduce.6.cloned.1.call-start = ((), (), s32[]{:S(2)}) async-start(), calls=%async_computation.3 | async-start | bytes 2097152 | tf_op jit(solution)/shard_map/psum | solution.py:21
  688.4 4.3 copy-start
  698.5 6.9 copy-start.1
  705.4 1.0 copy-start.3
  714.2 366.2 %reduce-scatter.2.cloned.1.call-start = ((), (), s32[]{:S(2)}) async-start(), calls=%async_computation.4 | async-start | bytes 9175040 | tf_op jit(solution)/shard_map/reduce_scatter | solution.py:40
  754.1 1.0 copy-start.5
  898.1 4.7 copy-start.4
  906.9 1.0 copy-start.2
  1015.2 119.9 %all-gather.5.cloned.1.call-start = ((), (), s32[]{:S(2)}) async-start(), calls=%async_computation.5 | async-start | bytes 9175040 | tf_op jit(solution)/shard_map/all_gather | solution.py:43
Sparse Core Ops, SparseCore 0:
  9.5 56.0 all-gather.2
  517.5 36.2 all-reduce.3
  714.3 36.7 all-reduce.5
  1015.3 65.0 reduce-scatter.1
  1081.8 53.2 all-gather.4
